TPU v7x, 32 devices: a whole 2x2x4 slice. The times are simulated.
32 devices in a mesh: grp: 4 (over y, x), tile: 8 (over z, core).
Axes of the slice: x: 2, y: 2, z: 4, core: 2. Of those that a mesh axis runs over, the one named last changes fastest.
Arguments:
- observed: bfloat16 [512, 32, 2048], P('tile', 'grp'), as said below
- visible: int32 [32, 2048], P('grp', 'tile'), may hold values from 0 to 65535
- params_start: float32 [8, 32, 2048], P(None, 'grp', 'tile'), may hold values from -1.5 to 1.5, as said below
- light_directions: float32 [3, 32], replicated, may hold values from -1 to 1
- view_dirs: float32 [3, 16], replicated, may hold values from -1 to 1
- gains_start: float32 [32], replicated, may hold values from 0.5 to 1.5
Outputs:
- params_out: float32 [8, 32, 2048], P(None, 'grp', 'tile')
- gains_out: float32 [32], replicated
Inputs may be any that keep to these rules, and one draw needn't show every extreme that they name: `observed`: luminance is positive. `params_start`: tilts within -0.3 to 0.3, diffuse 0.3 to 1.2, specular 0.1 to 0.8, sharpness logit -1.5 to 1.5, ambient -0.2 to 0.3, rim 0 to 0.5, retro -0.3 to 0.3.
All inputs are finite; a program needn't handle non-finite values.
Results may differ from a plain program's by a relative error of at most 0.0003.
Values may be sent and summed in bfloat16 or wider, within the bound.
No kernel may reach another device: no remote copies, remote signals or barrier semaphores. Data moves between devices by JAX's collectives and lax.ppermute only.
A program may use at most 64 MiB of HBM per device.

v0:
```python
import jax
import jax.numpy as jnp
from jax import lax
from jax.sharding import PartitionSpec as P

CAMS = 16
LIGHTS = 32
ITERS = 2
damping = 4.0
lift_z = 1.6


def padded_2(cells, sides, width):
    for axis, dim in sides:
        count = lax.axis_size(axis)
        ends = count - 1
        head = lax.slice_in_dim(cells, 0, width, axis=dim)
        tail = lax.slice_in_dim(cells, cells.shape[dim] - width, cells.shape[dim], axis=dim)
        cells = jnp.concatenate(
            [
                lax.ppermute(tail, axis, [(i, (i + 1) % count) for i in range(ends)]),
                cells,
                lax.ppermute(head, axis, [((i + 1) % count, i) for i in range(ends)]),
            ],
            axis=dim,
        )
    return cells


def unit_columns(raw):
    lifted = raw + jnp.array([0.0, 0.0, lift_z], jnp.float32)[:, None]
    return lifted / jnp.sqrt(jnp.sum(lifted * lifted, axis=0, keepdims=True))


def geometry(light_directions, view_dirs):
    lights = unit_columns(light_directions)
    views = unit_columns(view_dirs)
    raw_half = views.T[:, :, None] + lights[None]
    halves = raw_half / jnp.sqrt(jnp.sum(raw_half * raw_half, axis=1, keepdims=True))
    echoes = jnp.sum(views.T[:, :, None] * lights[None], axis=1)
    return (lights, halves, views.T, echoes)


def facing(dir_x, dir_y, dir_z, tilt_u, tilt_v, scale_q):
    facing_dot = (dir_x * tilt_u + dir_y * tilt_v + dir_z) * scale_q
    by_u = (dir_x - facing_dot * tilt_u * scale_q) * scale_q
    by_v = (dir_y - facing_dot * tilt_v * scale_q) * scale_q
    return (facing_dot, by_u, by_v)


def camera_terms(observed_c, weight_c, params, gains, lights, half_c, view_c, echo_c):
    tilt_u, tilt_v, diffuse, specular, sharp_raw, ambient, rim_gain, retro_gain = [
        params[i] for i in range(8)
    ]
    scale_q = 1.0 / jnp.sqrt(1.0 + tilt_u * tilt_u + tilt_v * tilt_v)
    light_dot, light_u, light_v = facing(
        lights[0][:, None], lights[1][:, None], lights[2][:, None], tilt_u, tilt_v, scale_q
    )
    half_dot, half_u, half_v = facing(
        half_c[0][:, None], half_c[1][:, None], half_c[2][:, None], tilt_u, tilt_v, scale_q
    )
    view_dot, view_u, view_v = facing(view_c[0], view_c[1], view_c[2], tilt_u, tilt_v, scale_q)
    sigma = jax.nn.sigmoid(sharp_raw)
    sharp = 1.0 + 20.0 * sigma
    lobe = jnp.exp(sharp * (half_dot - 1.0))
    back = 1.0 - view_dot
    rim_shape = back * back
    shaped = (
        diffuse * light_dot
        + specular * lobe
        + ambient
        + rim_gain * rim_shape
        + retro_gain * echo_c[:, None]
    )
    full = light_dot.shape
    jacob = [
        diffuse * light_u + specular * sharp * lobe * half_u - 2.0 * rim_gain * back * view_u,
        diffuse * light_v + specular * sharp * lobe * half_v - 2.0 * rim_gain * back * view_v,
        light_dot,
        lobe,
        specular * lobe * (half_dot - 1.0) * 20.0 * sigma * (1.0 - sigma),
        jnp.ones(full, jnp.float32),
        jnp.broadcast_to(rim_shape, full),
        jnp.broadcast_to(echo_c[:, None], full),
    ]
    column = gains[:, None]
    resid = observed_c.astype(jnp.float32) - column * shaped
    scaled = [column * piece for piece in jacob]
    surface_normal = []
    for i in range(8):
        for j in range(i, 8):
            surface_normal.append(weight_c * jnp.sum(scaled[i] * scaled[j], axis=0))
    right_side = [weight_c * jnp.sum(piece * resid, axis=0) for piece in scaled]
    lifted = jnp.sum(weight_c * shaped * resid, axis=1)
    energy = jnp.sum(weight_c * shaped * shaped, axis=1)
    return (jnp.stack(surface_normal), jnp.stack(right_side), lifted, energy)


def assemble(observed, weights, params, gains, lights, halves, views, echoes):
    texels = params.shape[1]

    def one_camera(carry, inputs):
        observed_c, weight_c, half_c, view_c, echo_c = inputs
        terms = camera_terms(observed_c, weight_c, params, gains, lights, half_c, view_c, echo_c)
        return (tuple((a + b for a, b in zip(carry, terms))), None)

    start = (
        jnp.zeros((36, texels), jnp.float32),
        jnp.zeros((8, texels), jnp.float32),
        jnp.zeros((LIGHTS,), jnp.float32),
        jnp.zeros((LIGHTS,), jnp.float32),
    )
    result, unused = lax.scan(one_camera, start, (observed, weights, halves, views, echoes))
    return result


def solve_eight(surface_normal, right_side):
    entries = {}
    where = 0
    for i in range(8):
        for j in range(i, 8):
            entries[i, j] = surface_normal[where]
            where += 1
    lower = {}
    for j in range(8):
        accum = entries[j, j] + damping
        for k in range(j):
            accum = accum - lower[j, k] * lower[j, k]
        root = jnp.sqrt(accum)
        lower[j, j] = root
        for i in range(j + 1, 8):
            accum = entries[j, i]
            for k in range(j):
                accum = accum - lower[i, k] * lower[j, k]
            lower[i, j] = accum / root
    forward = []
    for i in range(8):
        accum = right_side[i]
        for k in range(i):
            accum = accum - lower[i, k] * forward[k]
        forward.append(accum / lower[i, i])
    answer = [None] * 8
    for i in range(7, -1, -1):
        accum = forward[i]
        for k in range(i + 1, 8):
            accum = accum - lower[k, i] * answer[k]
        answer[i] = accum / lower[i, i]
    return jnp.stack(answer)


def smooth_tilts(tilt):
    rows = tilt.shape[1]
    cols = tilt.shape[2]
    padded = padded_2(tilt, (("grp", 1), ("tile", 2)), 1)
    boxed = jnp.zeros(tilt.shape, jnp.float32)
    for i in range(3):
        for j in range(3):
            boxed = boxed + padded[:, i : i + rows, j : j + cols]
    return 0.5 * tilt + boxed * (0.5 / 9.0)


def update_gains(gains, lifted, energy):
    totals = lax.psum(jnp.stack([lifted, energy]), ("grp", "tile"))
    return gains + totals[0] / (totals[1] + 1.0)


def on_device(observed, visible, params_start, light_directions, view_dirs, gains_start):
    lights, halves, views, echoes = geometry(light_directions, view_dirs)
    rows = visible.shape[0]
    cols = visible.shape[1]
    shifts = jnp.arange(CAMS, dtype=jnp.int32)
    weights = jnp.bitwise_and(jnp.right_shift(visible.reshape(1, -1), shifts[:, None]), 1).astype(
        jnp.float32
    )
    params = params_start.reshape(8, -1)
    gains = gains_start
    regrouped = lax.all_to_all(observed, "tile", split_axis=2, concat_axis=0, tiled=True)
    flat_obs = regrouped.reshape(CAMS, LIGHTS, rows * cols)
    first_terms = assemble(flat_obs, weights, params, gains, lights, halves, views, echoes)
    for iteration in range(ITERS):
        if iteration == 0:
            surface_normal, right_side, lifted, energy = first_terms
        else:
            surface_normal, right_side, lifted, energy = assemble(
                flat_obs, weights, params, gains, lights, halves, views, echoes
            )
        params = params + solve_eight(surface_normal, right_side)
        gains = update_gains(gains, lifted, energy)
        grid = params.reshape(8, rows, cols)
        params = jnp.concatenate([smooth_tilts(grid[:2]), grid[2:]], axis=0).reshape(8, -1)
    return (params.reshape(8, rows, cols), gains)


def solution(mesh):
    return jax.shard_map(
        on_device,
        mesh=mesh,
        in_specs=(P("tile", "grp", None), P("grp", "tile"), P(None, "grp", "tile"), P(), P(), P()),
        out_specs=(P(None, "grp", "tile"), P()),
        check_vma=False,
    )
```

profile of v0, /device:TPU:3, one launch (start us, length us, event | category | flops | bytes accessed | tf_op | source)
XLA Modules:
  0.0 603.4 jit_solution(8106772559715947173)
XLA Ops:
  0.6 6.7 %copy.16 = bf16[64,8,2048]{0,1,2:T(8,128)(2,1)} copy(bf16[64,8,2048]{2,1,0:T(8,128)(2,1)} %param.12) | data formatting | bytes 4194304 | tf_op args[0]
  7.3 7.6 %reshape.750 = bf16[8,2,65536]{2,1,0:T(2,128)(2,1)} reshape(bf16[2048,8,64]{2,1,0:T(8,128)(2,1)} %bitcast.458) | data formatting | bytes 4194304
  14.9 5.7 all-to-all-start
  22.1 46.7 %all-to-all-done = bf16[8,2,65536]{2,1,0:T(2,128)(2,1)S(1)} async-done(((bf16[8,2,65536]{2,1,0:T(2,128)(2,1)}), bf16[8,2,65536]{2,1,0:T(2,128)(2,1)S(1)}, u32[]{:S(2)}, u32[]{:S(2)}) %all-to-all-start) | async-done | bytes 2097184 | tf_op jit(solution)/shard_map/all_to_all | solution.py:177
  68.8 5.0 reshape.751
  73.8 5.0 copy.17
  81.2 201.9 %while.40 = (s32[]{:T(128)}, f32[36,2048]{1,0:T(8,128)S(1)}, f32[8,2048]{1,0:T(8,128)S(1)}, f32[32]{0:T(128)S(1)}, f32[32]{0:T(128)S(1)}, /*index=5*/f32[16,2048...) while((s32[]{:T(128)}, f32[36,2048]{1,0:T(8,128)S(1)}, ...), condition=%wide.region_51.52_spmd.clone, body=%wide.region_5.51_spmd.clone.sunk | while | flops 14035169 | bytes 4423358 | solution.py:113
  82.5 2.4 multiply_multiply_fusion.36
  95.1 2.4 multiply_multiply_fusion.36
  107.8 2.4 multiply_multiply_fusion.36
  120.4 2.4 multiply_multiply_fusion.36
  133.0 2.4 multiply_multiply_fusion.36
  145.6 2.4 multiply_multiply_fusion.36
  158.2 2.4 multiply_multiply_fusion.36
  170.8 2.4 multiply_multiply_fusion.36
  183.5 2.4 multiply_multiply_fusion.36
  233.9 2.4 multiply_multiply_fusion.36
  259.2 2.4 multiply_multiply_fusion.36
  284.9 3.1 collective-permute-start
  290.2 38.6 %psum.14 = f32[2,32]{1,0:T(2,128)S(1)} all-reduce(f32[2,32]{1,0:T(2,128)S(1)} %pad_maximum_fusion.10), channel_id=1, replica_groups=mesh['grp'=4,'tile'=8] {'grp','tile'}, use_global_device_ids=true, to_apply=%region_52.53 | all-reduce | flops 64 | bytes 512 | tf_op jit(solution)/shard_map/psum | solution.py:163
  329.5 5.9 collective-permute-start.2
  337.5 2.9 collective-permute-done.3
  340.8 203.1 %while.41 = (s32[]{:T(128)}, f32[36,2048]{1,0:T(8,128)S(1)}, f32[8,2048]{1,0:T(8,128)S(1)}, f32[32]{0:T(128)S(1)}, f32[32]{0:T(128)S(1)}, /*index=5*/f32[16,2048...) while((s32[]{:T(128)}, f32[36,2048]{1,0:T(8,128)S(1)}, ...), condition=%wide.region_100.101_spmd.clone, body=%wide.region_54.100_spmd.clone.sunk | while | flops 14035169 | bytes 4423358 | solution.py:113
  405.5 2.4 multiply_multiply_fusion.38
  418.2 2.4 multiply_multiply_fusion.38
  519.8 2.4 multiply_multiply_fusion.38
  532.5 2.4 multiply_multiply_fusion.38
  543.9 37.7 %psum.15 = f32[2,32]{1,0:T(2,128)S(1)} all-reduce(f32[2,32]{1,0:T(2,128)S(1)} %pad_maximum_fusion.11), channel_id=1, replica_groups=mesh['grp'=4,'tile'=8] {'grp','tile'}, use_global_device_ids=true, to_apply=%region_101.102 | all-reduce | flops 64 | bytes 512 | tf_op jit(solution)/shard_map/psum | solution.py:163
  583.3 3.1 collective-permute-start.4
  589.2 2.5 collective-permute-done.5
  591.7 5.8 collective-permute-start.6
  599.5 3.1 collective-permute-done.7
  (843 shorter events, 381.6 us)
Async XLA Ops:
  14.9 5.8 copy-start.3
  14.9 5.8 copy-start.5
  14.9 6.0 %copy-start.4 = (f32[3,32]{1,0:T(4,128)S(1)}, f32[3,32]{1,0:T(4,128)}, u32[]{:S(2)}) copy-start(f32[3,32]{1,0:T(4,128)} %param.15) | copy-start | bytes 1156
  14.9 6.4 %copy-start.1 = (f32[8,8,256]{2,1,0:T(8,128)S(1)}, f32[8,8,256]{2,1,0:T(8,128)}, u32[]{:S(2)}) copy-start(f32[8,8,256]{2,1,0:T(8,128)} %param.14) | copy-start | bytes 196612
  14.9 6.5 %copy-start.2 = (s32[8,256]{1,0:T(8,128)S(1)}, s32[8,256]{1,0:T(8,128)}, u32[]{:S(2)}) copy-start(s32[8,256]{1,0:T(8,128)} %param.13) | copy-start | bytes 24580
  14.9 6.5 %copy-start = (f32[32]{0:T(128)S(1)}, f32[32]{0:T(128)}, u32[]{:S(2)}) copy-start(f32[32]{0:T(128)} %param.17) | copy-start | bytes 388
  14.9 53.9 %all-to-all-start = ((bf16[8,2,65536]{2,1,0:T(2,128)(2,1)}), bf16[8,2,65536]{2,1,0:T(2,128)(2,1)S(1)}, u32[]{:S(2)}, u32[]{:S(2)}) async-start(bf16[8,2,65536]{2,1,0:T(2,128)(2,1)} %reshape.750), calls=%async_computation | async-start | bytes 4194304 | tf_op jit(solution)/shard_map/all_to_all | solution.py:177
  284.9 44.5 %collective-permute-start = (f32[2,1,256]{2,1,0:T(1,128)S(1)}, f32[2,1,256]{2,1,0:T(1,128)S(1)}, u32[]{:S(2)}, u32[]{:S(2)}) collective-permute-start(f32[2,1,256]{2,1,0:T(1,128)S(1)} %get-tuple-element.1093), channel_id=1, source_target_pairs={{0,8},{8,16},{16,24},{1,9},{9,17},{17,25},{2,10},{10,18},{18,26},{... | collective-permute-start | bytes 6152 | tf_op jit(solution)/shard_map/ppermute | solution.py:21
  288.0 41.4 %collective-permute-start.1 = (f32[2,1,256]{2,1,0:T(1,128)S(1)}, f32[2,1,256]{2,1,0:T(1,128)S(1)}, u32[]{:S(2)}, u32[]{:S(2)}) collective-permute-start(f32[2,1,256]{2,1,0:T(1,128)S(1)} %get-tuple-element.1094), channel_id=1, source_target_pairs={{8,0},{16,8},{24,16},{9,1},{17,9},{25,17},{10,2},{18,10},{26,18},{... | collective-permute-start | bytes 6152 | tf_op jit(solution)/shard_map/ppermute | solution.py:23
  329.5 8.0 %collective-permute-start.2 = (f32[2,10,1]{2,1,0:T(8,128)S(1)}, f32[2,10,1]{2,1,0:T(8,128)S(1)}, u32[]{:S(2)}, u32[]{:S(2)}) collective-permute-start(f32[2,10,1]{2,1,0:T(8,128)S(1)} %get-tuple-element.1081), channel_id=1, source_target_pairs={{0,1},{1,2},{2,3},{3,4},{4,5},{5,6},{6,7},{8,9},{9,10},{10,11},{11... | collective-permute-start | bytes 248 | tf_op jit(solution)/shard_map/ppermute | solution.py:21
  335.4 5.1 collective-permute-start.3
  583.3 5.9 collective-permute-start.4
  586.4 5.2 collective-permute-start.5
  591.7 7.8 %collective-permute-start.6 = (f32[2,10,1]{2,1,0:T(8,128)S(1)}, f32[2,10,1]{2,1,0:T(8,128)S(1)}, u32[]{:S(2)}, u32[]{:S(2)}) collective-permute-start(f32[2,10,1]{2,1,0:T(8,128)S(1)} %get-tuple-element.1079), channel_id=1, source_target_pairs={{0,1},{1,2},{2,3},{3,4},{4,5},{5,6},{6,7},{8,9},{9,10},{10,11},{11... | collective-permute-start | bytes 248 | tf_op jit(solution)/shard_map/ppermute | solution.py:21
  597.6 5.1 collective-permute-start.7
where the time goes:
time: 608 us; the launch traced here: 603 us
  other arithmetic  366 us (60%)
  blocking collectives  76.3 us (13%)
  local copies, waits for them, and re-layouts  67.8 us (11%)
  waiting for transfers between devices  55.2 us (9%)
  starting transfers between devices  32 us (5%)
    mul x32, other arithmetic, camera_terms(): 2.0 * rim_gain * back * view_v  78.1 us
    psum x2, blocking collectives, update_gains(): totals = lax.psum(jnp.stack([lifted, energy]), ('grp', 'tile'))  76.3 us
    reduce_sum x98, other arithmetic, camera_terms(): surface_normal.append(weight_c * jnp.sum(scaled[i] * scaled[j], axis=0))  61.1 us
    mul x32, other arithmetic, camera_terms(): rim_shape = back * back  57.2 us
    all_to_all x1, waiting for transfers between devices, on_device(): lax.all_to_all(observed, 'tile', split_axis=2, concat_axis=0, tiled=True)  46.7 us
    reduce_sum x32, other arithmetic, camera_terms(): lifted = jnp.sum(weight_c * shaped * resid, axis=1)  46.1 us
    mul x32, other arithmetic, camera_terms(): right_side = [weight_c * jnp.sum(piece * resid, axis=0) for piece in scaled]  43.2 us
    reduce_sum x32, other arithmetic, camera_terms(): right_side = [weight_c * jnp.sum(piece * resid, axis=0) for piece in scaled]  41.6 us
  transfers between devices with their start and end apart: 9, of which 4 were waited for; matrix products, arithmetic and copies ran while one was open for 0% of the time, Pallas kernels for 0%

commit v1 on v0

--- a/solution.py
+++ b/solution.py
@@ -174,7 +174,22 @@
     )
     params = params_start.reshape(8, -1)
     gains = gains_start
-    regrouped = lax.all_to_all(observed, "tile", split_axis=2, concat_axis=0, tiled=True)
+    arr_next, after = (lax.axis_size("tile"), lax.axis_index("tile"))
+    z = list(observed.shape)
+    later = observed.shape[2] // arr_next
+    z[2] = later
+    block_last = z[0]
+    z[0] = block_last * arr_next
+    regrouped = jnp.zeros(z, observed.dtype)
+    for jj in range(arr_next):
+        outer = lax.dynamic_slice_in_dim(observed, (after ^ jj) * later, later, axis=2)
+        if jj:
+            outer = lax.ppermute(
+                outer, axis_name="tile", perm=[(dev_j, dev_j ^ jj) for dev_j in range(arr_next)]
+            )
+        regrouped = lax.dynamic_update_slice_in_dim(
+            regrouped, outer, (after ^ jj) * block_last, axis=0
+        )
     flat_obs = regrouped.reshape(CAMS, LIGHTS, rows * cols)
     first_terms = assemble(flat_obs, weights, params, gains, lights, halves, views, echoes)
     for iteration in range(ITERS):

time: 608 us -> 587 us (0.965)
  waiting for transfers between devices: 55.2 us -> 30.5 us
  local copies, waits for them, and re-layouts: 67.8 us -> 51.3 us
  blocking collectives: 76.3 us -> 89.6 us
    all_to_all x1 -> x0, waiting for transfers between devices: 46.7 us -> none  [on_device(): lax.all_to_all(observed, 'tile', split_axis=2, concat_axis=0, tiled=True)]
    ppermute x0 -> x7, waiting for transfers between devices: none -> 24.2 us  [on_device(): lax.ppermute(outer, axis_name='tile', perm=[(dev_j, dev_j ^ jj) for dev_j...]
    unnamed x30 -> x29, local copies, waits for them, and re-layouts: 19.4 us -> 1.6 us
    psum x2, blocking collectives: 76.3 us -> 89.6 us  [update_gains(): totals = lax.psum(jnp.stack([lifted, energy]), ('grp', 'tile'))]
    ppermute x0 -> x7, starting transfers between devices: none -> 10.7 us  [on_device(): lax.ppermute(outer, axis_name='tile', perm=[(dev_j, dev_j ^ jj) for dev_j...]
  transfers between devices with their start and end apart: 9 -> 15, of which waited for: 4 -> 6; matrix products, arithmetic and copies ran while one was open for 0% -> 1% of each run, Pallas kernels for 0% -> 0%
where the time goes in v1:
time: 587 us; the launch traced here: 582 us
  other arithmetic  369 us (63%)
  blocking collectives  89.6 us (15%)
  local copies, waits for them, and re-layouts  51.3 us (9%)
  starting transfers between devices  35.6 us (6%)
  waiting for transfers between devices  30.5 us (5%)
    psum x2, blocking collectives, update_gains(): totals = lax.psum(jnp.stack([lifted, energy]), ('grp', 'tile'))  89.6 us
    mul x32, other arithmetic, camera_terms(): 2.0 * rim_gain * back * view_v  78.2 us
    reduce_sum x98, other arithmetic, camera_terms(): surface_normal.append(weight_c * jnp.sum(scaled[i] * scaled[j], axis=0))  61.4 us
    mul x32, other arithmetic, camera_terms(): rim_shape = back * back  57.2 us
    reduce_sum x32, other arithmetic, camera_terms(): lifted = jnp.sum(weight_c * shaped * resid, axis=1)  46.3 us
    mul x32, other arithmetic, camera_terms(): right_side = [weight_c * jnp.sum(piece * resid, axis=0) for piece in scaled]  44.8 us
    reduce_sum x32, other arithmetic, camera_terms(): right_side = [weight_c * jnp.sum(piece * resid, axis=0) for piece in scaled]  42.4 us
    ppermute x7, waiting for transfers between devices, on_device(): lax.ppermute(outer, axis_name='tile', perm=[(dev_j, dev_j ^ jj) for dev_j...  24.2 us
  transfers between devices with their start and end apart: 15, of which 6 were waited for; matrix products, arithmetic and copies ran while one was open for 1% of the time, Pallas kernels for 0%

profile of v1, /device:TPU:3, one launch (start us, length us, event | category | flops | bytes accessed | tf_op | source)
XLA Modules:
  0.0 582.0 jit_solution(6742043659297808587)
XLA Ops:
  10.3 3.4 collective-permute-start.5
  14.6 8.6 %collective-permute-done.1 = bf16[64,8,256]{2,1,0:T(8,128)(2,1)} collective-permute-done((bf16[64,8,256]{2,1,0:T(8,128)(2,1)}, bf16[64,8,256]{2,1,0:T(8,128)(2,1)}, u32[]{:S(2)}, u32[]{:S(2)}) %collective-permute-start.1) | collective-permute-done | bytes 262176 | tf_op jit(solution)/shard_map/ppermute | solution.py:187
  26.4 2.5 collective-permute-done.2
  30.9 13.0 %collective-permute-done.4 = bf16[64,8,256]{2,1,0:T(8,128)(2,1)} collective-permute-done((bf16[64,8,256]{2,1,0:T(8,128)(2,1)}, bf16[64,8,256]{2,1,0:T(8,128)(2,1)}, u32[]{:S(2)}, u32[]{:S(2)}) %collective-permute-start.4) | collective-permute-done | bytes 262176 | tf_op jit(solution)/shard_map/ppermute | solution.py:187
  47.4 204.0 %while.40 = (s32[]{:T(128)}, f32[36,2048]{1,0:T(8,128)S(1)}, f32[8,2048]{1,0:T(8,128)S(1)}, f32[32]{0:T(128)S(1)}, f32[32]{0:T(128)S(1)}, /*index=5*/f32[16,2048...) while((s32[]{:T(128)}, f32[36,2048]{1,0:T(8,128)S(1)}, ...), condition=%wide.region_51.52_spmd.clone, body=%wide.region_5.51_spmd.clone.sunk | while | flops 14035169 | bytes 4423358 | solution.py:113
  74.2 2.4 multiply_multiply_fusion.36
  112.4 2.4 multiply_multiply_fusion.36
  253.2 3.1 collective-permute-start.7
  258.5 49.9 %psum.14 = f32[2,32]{1,0:T(2,128)S(1)} all-reduce(f32[2,32]{1,0:T(2,128)S(1)} %pad_maximum_fusion.10), channel_id=1, replica_groups=mesh['grp'=4,'tile'=8] {'grp','tile'}, use_global_device_ids=true, to_apply=%region_52.53 | all-reduce | flops 64 | bytes 512 | tf_op jit(solution)/shard_map/psum | solution.py:163
  309.1 3.4 collective-permute-start.10
  315.9 203.6 %while.41 = (s32[]{:T(128)}, f32[36,2048]{1,0:T(8,128)S(1)}, f32[8,2048]{1,0:T(8,128)S(1)}, f32[32]{0:T(128)S(1)}, f32[32]{0:T(128)S(1)}, /*index=5*/f32[16,2048...) while((s32[]{:T(128)}, f32[36,2048]{1,0:T(8,128)S(1)}, ...), condition=%wide.region_100.101_spmd.clone, body=%wide.region_54.100_spmd.clone.sunk | while | flops 14035169 | bytes 4423358 | solution.py:113
  317.2 2.4 multiply_multiply_fusion.38
  330.0 2.4 multiply_multiply_fusion.38
  342.7 2.4 multiply_multiply_fusion.38
  355.4 2.4 multiply_multiply_fusion.38
  368.1 2.4 multiply_multiply_fusion.38
  380.9 2.4 multiply_multiply_fusion.38
  393.6 2.4 multiply_multiply_fusion.38
  406.3 2.4 multiply_multiply_fusion.38
  419.1 2.4 multiply_multiply_fusion.38
  431.8 2.4 multiply_multiply_fusion.38
  444.5 2.4 multiply_multiply_fusion.38
  457.2 2.4 multiply_multiply_fusion.38
  470.0 2.4 multiply_multiply_fusion.38
  482.7 2.4 multiply_multiply_fusion.38
  495.4 2.4 multiply_multiply_fusion.38
  508.1 2.4 multiply_multiply_fusion.38
  519.6 39.7 %psum.15 = f32[2,32]{1,0:T(2,128)S(1)} all-reduce(f32[2,32]{1,0:T(2,128)S(1)} %pad_maximum_fusion.11), channel_id=1, replica_groups=mesh['grp'=4,'tile'=8] {'grp','tile'}, use_global_device_ids=true, to_apply=%region_101.102 | all-reduce | flops 64 | bytes 512 | tf_op jit(solution)/shard_map/psum | solution.py:163
  561.0 3.1 collective-permute-start.11
  566.9 2.5 collective-permute-done.12
  569.4 6.7 %collective-permute-start.13 = (f32[2,10,1]{2,1,0:T(8,128)S(1)}, f32[2,10,1]{2,1,0:T(8,128)S(1)}, u32[]{:S(2)}, u32[]{:S(2)}) collective-permute-start(f32[2,10,1]{2,1,0:T(8,128)S(1)} %get-tuple-element.1087), channel_id=1, source_target_pairs={{0,1},{1,2},{2,3},{3,4},{4,5},{5,6},{6,7},{8,9},{9,10},{10,11},{11... | collective-permute-start | bytes 248 | tf_op jit(solution)/shard_map/ppermute | solution.py:21
  578.1 3.1 collective-permute-done.14
  (862 shorter events, 393.1 us)
Async XLA Ops:
  0.7 1.6 copy-start
  2.3 6.4 %copy-start.4 = (f32[3,16]{1,0:T(4,128)S(1)}, f32[3,16]{1,0:T(4,128)}, u32[]{:S(2)}) copy-start(f32[3,16]{1,0:T(4,128)} %param.16) | copy-start | bytes 580
  2.3 6.4 %copy-start.6 = (f32[3]{0:T(128)S(1)}, f32[3]{0:T(128)}, u32[]{:S(2)}) copy-start(f32[3]{0:T(128)} %constant.155.clone) | copy-start | bytes 40
  2.3 6.7 %copy-start.5 = (f32[3,32]{1,0:T(4,128)S(1)}, f32[3,32]{1,0:T(4,128)}, u32[]{:S(2)}) copy-start(f32[3,32]{1,0:T(4,128)} %param.15) | copy-start | bytes 1156
  2.3 7.1 %copy-start.3 = (s32[8,256]{1,0:T(8,128)S(1)}, s32[8,256]{1,0:T(8,128)}, u32[]{:S(2)}) copy-start(s32[8,256]{1,0:T(8,128)} %param.13) | copy-start | bytes 24580
  2.3 7.1 %copy-start.2 = (f32[8,8,256]{2,1,0:T(8,128)S(1)}, f32[8,8,256]{2,1,0:T(8,128)}, u32[]{:S(2)}) copy-start(f32[8,8,256]{2,1,0:T(8,128)} %param.14) | copy-start | bytes 196612
  2.3 7.1 %copy-start.1 = (f32[32]{0:T(128)S(1)}, f32[32]{0:T(128)}, u32[]{:S(2)}) copy-start(f32[32]{0:T(128)} %param.17) | copy-start | bytes 388
  3.6 6.6 %collective-permute-start = (bf16[64,8,256]{2,1,0:T(8,128)(2,1)}, bf16[64,8,256]{2,1,0:T(8,128)(2,1)}, u32[]{:S(2)}, u32[]{:S(2)}) collective-permute-start(bf16[64,8,256]{2,1,0:T(8,128)(2,1)} %get-tuple-element.1079), channel_id=1, source_target_pairs={{0,1},{1,0},{2,3},{3,2},{4,5},{5,4},{6,7},{7,6},{8,9},{9,8},{10,11... | collective-permute-start | bytes 786440 | tf_op jit(solution)/shard_map/ppermute | solution.py:187
  4.3 18.9 %collective-permute-start.1 = (bf16[64,8,256]{2,1,0:T(8,128)(2,1)}, bf16[64,8,256]{2,1,0:T(8,128)(2,1)}, u32[]{:S(2)}, u32[]{:S(2)}) collective-permute-start(bf16[64,8,256]{2,1,0:T(8,128)(2,1)} %get-tuple-element.1078), channel_id=1, source_target_pairs={{0,2},{1,3},{2,0},{3,1},{4,6},{5,7},{6,4},{7,5},{8,10},{9,11},{10,... | collective-permute-start | bytes 786440 | tf_op jit(solution)/shard_map/ppermute | solution.py:187
  5.6 23.4 %collective-permute-start.2 = (bf16[64,8,256]{2,1,0:T(8,128)(2,1)}, bf16[64,8,256]{2,1,0:T(8,128)(2,1)}, u32[]{:S(2)}, u32[]{:S(2)}) collective-permute-start(bf16[64,8,256]{2,1,0:T(8,128)(2,1)} %get-tuple-element.1077), channel_id=1, source_target_pairs={{0,3},{1,2},{2,1},{3,0},{4,7},{5,6},{6,5},{7,4},{8,11},{9,10},{10,... | collective-permute-start | bytes 786440 | tf_op jit(solution)/shard_map/ppermute | solution.py:187
  5.9 24.0 %collective-permute-start.3 = (bf16[64,8,256]{2,1,0:T(8,128)(2,1)}, bf16[64,8,256]{2,1,0:T(8,128)(2,1)}, u32[]{:S(2)}, u32[]{:S(2)}) collective-permute-start(bf16[64,8,256]{2,1,0:T(8,128)(2,1)} %get-tuple-element.1076), channel_id=1, source_target_pairs={{0,4},{1,5},{2,6},{3,7},{4,0},{5,1},{6,2},{7,3},{8,12},{9,13},{10,... | collective-permute-start | bytes 786440 | tf_op jit(solution)/shard_map/ppermute | solution.py:187
  8.2 35.7 %collective-permute-start.4 = (bf16[64,8,256]{2,1,0:T(8,128)(2,1)}, bf16[64,8,256]{2,1,0:T(8,128)(2,1)}, u32[]{:S(2)}, u32[]{:S(2)}) collective-permute-start(bf16[64,8,256]{2,1,0:T(8,128)(2,1)} %get-tuple-element.1075), channel_id=1, source_target_pairs={{0,5},{1,4},{2,7},{3,6},{4,1},{5,0},{6,3},{7,2},{8,13},{9,12},{10,... | collective-permute-start | bytes 786440 | tf_op jit(solution)/shard_map/ppermute | solution.py:187
  10.3 34.7 %collective-permute-start.5 = (bf16[64,8,256]{2,1,0:T(8,128)(2,1)}, bf16[64,8,256]{2,1,0:T(8,128)(2,1)S(1)}, u32[]{:S(2)}, u32[]{:S(2)}) collective-permute-start(bf16[64,8,256]{2,1,0:T(8,128)(2,1)} %get-tuple-element.1081), channel_id=1, source_target_pairs={{0,6},{1,7},{2,4},{3,5},{4,2},{5,3},{6,0},{7,1},{8,14},{9,15},{10,... | collective-permute-start | bytes 786440 | tf_op jit(solution)/shard_map/ppermute | solution.py:187
  23.2 21.7 %collective-permute-start.6 = (bf16[64,8,256]{2,1,0:T(8,128)(2,1)S(1)}, bf16[64,8,256]{2,1,0:T(8,128)(2,1)S(1)}, u32[]{:S(2)}, u32[]{:S(2)}) collective-permute-start(bf16[64,8,256]{2,1,0:T(8,128)(2,1)S(1)} %get-tuple-element.1074), channel_id=1, source_target_pairs={{0,7},{1,6},{2,5},{3,4},{4,3},{5,2},{6,1},{7,0},{8,15},{9,14},{10,... | collective-permute-start | bytes 786440 | tf_op jit(solution)/shard_map/ppermute | solution.py:187
  253.2 55.9 %collective-permute-start.7 = (f32[2,1,256]{2,1,0:T(1,128)S(1)}, f32[2,1,256]{2,1,0:T(1,128)S(1)}, u32[]{:S(2)}, u32[]{:S(2)}) collective-permute-start(f32[2,1,256]{2,1,0:T(1,128)S(1)} %get-tuple-element.1101), channel_id=1, source_target_pairs={{0,8},{8,16},{16,24},{1,9},{9,17},{17,25},{2,10},{10,18},{18,26},{... | collective-permute-start | bytes 6152 | tf_op jit(solution)/shard_map/ppermute | solution.py:21
  256.3 52.7 %collective-permute-start.8 = (f32[2,1,256]{2,1,0:T(1,128)S(1)}, f32[2,1,256]{2,1,0:T(1,128)S(1)}, u32[]{:S(2)}, u32[]{:S(2)}) collective-permute-start(f32[2,1,256]{2,1,0:T(1,128)S(1)} %get-tuple-element.1102), channel_id=1, source_target_pairs={{8,0},{16,8},{24,16},{9,1},{17,9},{25,17},{10,2},{18,10},{26,18},{... | collective-permute-start | bytes 6152 | tf_op jit(solution)/shard_map/ppermute | solution.py:23
  309.1 5.8 collective-permute-start.10
  312.5 3.1 collective-permute-start.9
  561.0 5.9 %collective-permute-start.11 = (f32[2,1,256]{2,1,0:T(1,128)S(1)}, f32[2,1,256]{2,1,0:T(1,128)S(1)}, u32[]{:S(2)}, u32[]{:S(2)}) collective-permute-start(f32[2,1,256]{2,1,0:T(1,128)S(1)} %get-tuple-element.1095), channel_id=1, source_target_pairs={{0,8},{8,16},{16,24},{1,9},{9,17},{17,25},{2,10},{10,18},{18,26},{... | collective-permute-start | bytes 6152 | tf_op jit(solution)/shard_map/ppermute | solution.py:21
  564.1 5.2 collective-permute-start.12
  569.4 8.7 %collective-permute-start.13 = (f32[2,10,1]{2,1,0:T(8,128)S(1)}, f32[2,10,1]{2,1,0:T(8,128)S(1)}, u32[]{:S(2)}, u32[]{:S(2)}) collective-permute-start(f32[2,10,1]{2,1,0:T(8,128)S(1)} %get-tuple-element.1087), channel_id=1, source_target_pairs={{0,1},{1,2},{2,3},{3,4},{4,5},{5,6},{6,7},{8,9},{9,10},{10,11},{11... | collective-permute-start | bytes 248 | tf_op jit(solution)/shard_map/ppermute | solution.py:21
  576.2 5.1 collective-permute-start.14
